TPU v7x, 512 devices: a whole 4x8x8 slice. The times are simulated.
512 devices in a mesh: wide: 128 (over y, z, core), narrow: 4 (over x).
Axes of the slice: x: 4, y: 8, z: 8, core: 2. Of those that a mesh axis runs over, the one named last changes fastest.
Arguments:
- grad_out: bfloat16 [32768, 512], P('wide', 'narrow'), may hold values from -24 to 24
- relu_mask: int32 [32768, 512], P('wide', 'narrow'), may hold values 0 or 1
- features: bfloat16 [32768, 512], P('wide', 'narrow'), may hold values from -6 to 6
- hop1_mean: bfloat16 [32768, 512], P('wide', 'narrow'), may hold values from -6 to 6
- hop2_mean: bfloat16 [32768, 512], P('wide', 'narrow'), may hold values from -6 to 6
- w_self: bfloat16 [512, 512], P('narrow'), may hold values from -0.25 to 0.25
- w_hop1: bfloat16 [512, 512], P('narrow'), may hold values from -0.25 to 0.25
- w_hop2: bfloat16 [512, 512], P('narrow'), may hold values from -0.25 to 0.25
- norm: float32 [32768], P('wide'), may hold values from 0.05 to 1
- tile_src: int32 [16384], P('wide'), may hold values from 0 to 1
- tile_owner: int32 [16384], P('wide'), may hold values from 0 to 127, as said below
- tile_block: int32 [16384], P('wide'), may hold values from 0 to 1
- tile_cols: int32 [16384, 128, 8], P('wide'), may hold values from 0 to 127
Outputs:
- grad_features: bfloat16 [32768, 512], P('wide', 'narrow')
- weight_grads: float32 [3, 512, 512], P(None, 'wide', 'narrow')
Inputs may be any that keep to these rules, and one draw needn't show every extreme that they name: `tile_owner`: the 128 tiles of one device name every device once as owner.
All inputs are finite; a program needn't handle non-finite values. No bound on the sum of `relu_mask` on one device may be relied on, other than what follows from the above.
Results may differ from a plain program's by a relative error of at most 0.0054.
Values may be sent and summed in bfloat16 or wider, within the bound.
No kernel may reach another device: no remote copies, remote signals or barrier semaphores. Data moves between devices by JAX's collectives and lax.ppermute only.
A program may use at most 64 MiB of HBM per device.

v0:
```python
import jax
import jax.numpy as jnp
from jax import lax
from jax.sharding import PartitionSpec as P


def tile_pattern(tile_cols):
    positions = jnp.arange(tile_cols.shape[1], dtype=jnp.int32)
    summed = jnp.zeros(tile_cols.shape[:2] + (tile_cols.shape[1],), jnp.int32)
    for column in range(tile_cols.shape[2]):
        summed = summed + (tile_cols[:, :, column, None] == positions).astype(jnp.int32)
    return summed.astype(jnp.bfloat16)


def on_device(
    grad_out,
    relu_mask,
    features,
    hop1_mean,
    hop2_mean,
    w_self,
    w_hop1,
    w_hop2,
    norm,
    tile_src,
    tile_owner,
    tile_block,
    tile_cols,
):
    node_count = features.shape[0]
    local_width = features.shape[1]
    block_rows = tile_cols.shape[1]
    row_blocks = node_count // block_rows
    owner_count = lax.axis_size("wide")
    gated = grad_out * relu_mask.astype(jnp.bfloat16)
    gated_full = lax.all_gather(gated, "narrow", axis=1, tiled=True)
    row_scale = norm[:, None]
    slot_ids = jnp.full((owner_count, 1), -1.0, jnp.float32)
    slot_ids = slot_ids.at[tile_owner, 0].set(tile_block.astype(jnp.float32)).astype(jnp.bfloat16)
    block_marks = jnp.arange(row_blocks, dtype=jnp.float32).astype(jnp.bfloat16)

    def combine_arrived(arrived, arrived_ids):
        select = (arrived_ids[:, 0][None, :] == block_marks[:, None]).astype(jnp.bfloat16)
        summed = jnp.einsum("bs,sjd->bjd", select, arrived, preferred_element_type=jnp.float32)
        return summed.reshape(node_count, local_width)

    pattern = tile_pattern(tile_cols)

    def transpose_hop(scaled):
        picked = scaled.reshape(row_blocks, block_rows, local_width)[tile_src]
        products = jnp.einsum(
            "trj,trd->tjd", pattern, picked, preferred_element_type=jnp.float32
        ).astype(jnp.bfloat16)
        outgoing = (
            jnp.zeros((owner_count, block_rows, local_width), jnp.bfloat16)
            .at[tile_owner]
            .set(products)
        )
        arrived, arrived_ids = (
            lax.all_to_all(outgoing, "wide", split_axis=0, concat_axis=0, tiled=True),
            lax.all_to_all(slot_ids, "wide", split_axis=0, concat_axis=0, tiled=True),
        )
        return combine_arrived(arrived, arrived_ids)

    def project(weight):
        return lax.dot_general(
            gated_full, weight, (((1,), (1,)), ((), ())), preferred_element_type=jnp.float32
        )

    scaled2 = (row_scale * project(w_hop2)).astype(jnp.bfloat16)
    agg2 = transpose_hop(scaled2)
    scaled1 = (row_scale * (project(w_hop1) + agg2)).astype(jnp.bfloat16)
    agg1 = transpose_hop(scaled1)
    grad_features = (project(w_self) + agg1).astype(jnp.bfloat16)
    partial_grads = jnp.stack(
        [
            jnp.einsum("ro,rd->od", gated_full, operand, preferred_element_type=jnp.float32)
            for operand in (features, hop1_mean, hop2_mean)
        ]
    )
    weight_grads = lax.psum_scatter(partial_grads, "wide", scatter_dimension=1, tiled=True)
    return (grad_features, weight_grads)


def solution(mesh):
    placed = (
        P("wide", "narrow"),
        P("wide", "narrow"),
        P("wide", "narrow"),
        P("wide", "narrow"),
        P("wide", "narrow"),
        P("narrow", None),
        P("narrow", None),
        P("narrow", None),
        P("wide"),
        P("wide"),
        P("wide"),
        P("wide"),
        P("wide", None, None),
    )
    return jax.shard_map(
        on_device,
        mesh=mesh,
        in_specs=placed,
        out_specs=(P("wide", "narrow"), P(None, "wide", "narrow")),
        check_vma=False,
    )
```

profile of v0, /device:TPU:24, one launch (start us, length us, event | category | flops | bytes accessed | tf_op | source)
XLA Modules:
  0.0 538.8 jit_solution(16396398977169809282)
XLA Ops:
  8.5 1.0 scatter_custom_fusion
  10.3 17.3 %all-to-all-start = ((bf16[128,1,1]{2,1,0:T(2,128)(2,1)}), bf16[128,1,1]{2,1,0:T(2,128)(2,1)S(1)}, u32[]{:S(2)}, u32[]{:S(2)}) async-start(bf16[128,1,1]{2,1,0:T(2,128)(2,1)} %copy.26), calls=%async_computation | async-start | bytes 131072 | tf_op jit(solution)/shard_map/all_to_all | solution.py:61
  27.6 3.4 fusion.18
  31.1 1.0 convert_multiply_fusion
  32.0 11.9 %all_gather.3 = bf16[256,512]{1,0:T(8,128)(2,1)S(1)} all-gather(bf16[256,128]{1,0:T(8,128)(2,1)S(1)} %convert_multiply_fusion), channel_id=1, replica_groups=mesh['wide'=128,'narrow'=4] {'narrow'}, dimensions={1}, use_global_device_ids=true | all-gather | bytes 327680 | tf_op jit(solution)/shard_map/all_gather | solution.py:36
  44.6 0.9 fusion.7
  45.6 3.1 gather_fusion
  48.6 12.0 %convolution_convert_fusion.1 = bf16[128,128,128]{2,1,0:T(8,128)(2,1)} fusion(bf16[128,128,128]{2,1,0:T(8,128)(2,1)} %gather_fusion, s32[128,128]{1,0:T(8,128)S(1)} %bitcast.58, s32[128,128]{1,0:T(8,128)S(1)} %bitcast.60, s32[128,128]{1,0:T(8,128)S(1)} %bitcast.48, s32[128,128]{1,0:T(8,128)S(1)} %bitcast.50, s32[128,128]{1,0:T(8,128)S(1)} %bitcast.52, ...), kind=kOutput, calls=%fused_computation.19 | convolution fusion | flops 589299712 | bytes 8912896 | tf_op jit(solution)/shard_map/trj,trd->tjd/dot_general | solution.py:51
  60.6 3.0 broadcast.17.clone
  63.7 19.4 %scatter_fusion = bf16[128,128,128]{2,1,0:T(8,128)(2,1)} fusion(bf16[128,128,128]{2,1,0:T(8,128)(2,1)} %broadcast.17.clone, s32[128]{0:T(128)S(1)} %compare_select_fusion.1, bf16[128,128,128]{2,1,0:T(8,128)(2,1)} %convolution_convert_fusion.1), kind=kCustom, calls=%fused_computation.3 | custom fusion | bytes 12583424 | tf_op jit(solution)/shard_map/scatter | solution.py:57
  83.0 14.2 %all-to-all-start.1 = ((bf16[128,128,128]{2,1,0:T(8,128)(2,1)}), bf16[128,128,128]{2,1,0:T(8,128)(2,1)}, u32[]{:S(2)}, u32[]{:S(2)}) async-start(bf16[128,128,128]{2,1,0:T(8,128)(2,1)} %scatter_fusion), calls=%async_computation.1 | async-start | bytes 8388608 | tf_op jit(solution)/shard_map/all_to_all | solution.py:60
  97.3 1.0 reduce
  98.3 99.9 %all-to-all-done.1 = bf16[128,128,128]{2,1,0:T(8,128)(2,1)} async-done(((bf16[128,128,128]{2,1,0:T(8,128)(2,1)}), bf16[128,128,128]{2,1,0:T(8,128)(2,1)}, u32[]{:S(2)}, u32[]{:S(2)}) %all-to-all-start.1) | async-done | bytes 4194336 | tf_op jit(solution)/shard_map/all_to_all | solution.py:60
  198.2 4.5 fusion.2
  202.9 3.1 gather_fusion.1
  206.0 12.0 %convolution_convert_fusion = bf16[128,128,128]{2,1,0:T(8,128)(2,1)} fusion(bf16[128,128,128]{2,1,0:T(8,128)(2,1)} %gather_fusion.1, s32[128,128]{1,0:T(8,128)S(1)} %bitcast.59, s32[128,128]{1,0:T(8,128)S(1)} %bitcast.61, s32[128,128]{1,0:T(8,128)S(1)} %bitcast.49, s32[128,128]{1,0:T(8,128)S(1)} %bitcast.51, s32[128,128]{1,0:T(8,128)S(1)} %bitcast.53, ...), kind=kOutput, calls=%fused_computation.18 | convolution fusion | flops 589299712 | bytes 8912896 | tf_op jit(solution)/shard_map/trj,trd->tjd/dot_general | solution.py:51
  218.0 3.0 broadcast.17
  221.0 19.4 %scatter_fusion.1 = bf16[128,128,128]{2,1,0:T(8,128)(2,1)} fusion(bf16[128,128,128]{2,1,0:T(8,128)(2,1)} %broadcast.17, s32[128]{0:T(128)S(1)} %compare_select_fusion.1, bf16[128,128,128]{2,1,0:T(8,128)(2,1)} %convolution_convert_fusion), kind=kCustom, calls=%fused_computation.4 | custom fusion | bytes 12583424 | tf_op jit(solution)/shard_map/scatter | solution.py:57
  240.4 11.5 %all-to-all-start.2 = ((bf16[128,128,128]{2,1,0:T(8,128)(2,1)}), bf16[128,128,128]{2,1,0:T(8,128)(2,1)}, u32[]{:S(2)}, u32[]{:S(2)}) async-start(bf16[128,128,128]{2,1,0:T(8,128)(2,1)} %scatter_fusion.1), calls=%async_computation.2 | async-start | bytes 8388608 | tf_op jit(solution)/shard_map/all_to_all | solution.py:60
  253.0 0.9 pad_maximum_fusion
  253.9 1.3 dynamic-slice
  255.9 269.4 %all-reduce.4.cloned.1.call-done = f32[3,512,128]{2,1,0:T(8,128)} async-done(((f32[3,512,128]{2,1,0:T(8,128)}), f32[3,512,128]{2,1,0:T(8,128)}) %all-reduce.4.cloned.1.call-update) | async-done | bytes 786448
  525.3 1.3 constant_dynamic-slice_fusion
  526.6 4.5 fusion
  (32 shorter events, 5.0 us)
Async XLA Ops:
  7.2 37.5 %copy-start = (bf16[128,512]{1,0:T(8,128)(2,1)S(1)}, bf16[128,512]{1,0:T(8,128)(2,1)}, u32[]{:S(2)}) copy-start(bf16[128,512]{1,0:T(8,128)(2,1)} %param.20) | copy-start | bytes 393220
  10.3 72.7 %all-to-all-start = ((bf16[128,1,1]{2,1,0:T(2,128)(2,1)}), bf16[128,1,1]{2,1,0:T(2,128)(2,1)S(1)}, u32[]{:S(2)}, u32[]{:S(2)}) async-start(bf16[128,1,1]{2,1,0:T(2,128)(2,1)} %copy.26), calls=%async_computation | async-start | bytes 131072 | tf_op jit(solution)/shard_map/all_to_all | solution.py:61
  83.0 115.1 %all-to-all-start.1 = ((bf16[128,128,128]{2,1,0:T(8,128)(2,1)}), bf16[128,128,128]{2,1,0:T(8,128)(2,1)}, u32[]{:S(2)}, u32[]{:S(2)}) async-start(bf16[128,128,128]{2,1,0:T(8,128)(2,1)} %scatter_fusion), calls=%async_computation.1 | async-start | bytes 8388608 | tf_op jit(solution)/shard_map/all_to_all | solution.py:60
  97.2 105.4 %copy-start.1 = (bf16[128,512]{1,0:T(8,128)(2,1)S(1)}, bf16[128,512]{1,0:T(8,128)(2,1)}, u32[]{:S(2)}) copy-start(bf16[128,512]{1,0:T(8,128)(2,1)} %param.19) | copy-start | bytes 393220
  97.3 105.4 %copy-start.6 = (f32[256]{0:T(256)S(1)}, f32[256]{0:T(256)}, u32[]{:S(2)}) copy-start(f32[256]{0:T(256)} %param.21) | copy-start | bytes 3076
  240.4 11.8 %copy-start.3 = (bf16[256,128]{1,0:T(8,128)(2,1)S(1)}, bf16[256,128]{1,0:T(8,128)(2,1)}, u32[]{:S(2)}) copy-start(bf16[256,128]{1,0:T(8,128)(2,1)} %param.17) | copy-start | bytes 196612
  240.4 12.1 %copy-start.4 = (bf16[256,128]{1,0:T(8,128)(2,1)S(1)}, bf16[256,128]{1,0:T(8,128)(2,1)}, u32[]{:S(2)}) copy-start(bf16[256,128]{1,0:T(8,128)(2,1)} %param.16) | copy-start | bytes 196612
  240.4 12.3 %copy-start.5 = (bf16[256,128]{1,0:T(8,128)(2,1)S(1)}, bf16[256,128]{1,0:T(8,128)(2,1)}, u32[]{:S(2)}) copy-start(bf16[256,128]{1,0:T(8,128)(2,1)} %param.15) | copy-start | bytes 196612
  240.4 286.2 %all-to-all-start.2 = ((bf16[128,128,128]{2,1,0:T(8,128)(2,1)}), bf16[128,128,128]{2,1,0:T(8,128)(2,1)}, u32[]{:S(2)}, u32[]{:S(2)}) async-start(bf16[128,128,128]{2,1,0:T(8,128)(2,1)} %scatter_fusion.1), calls=%async_computation.2 | async-start | bytes 8388608 | tf_op jit(solution)/shard_map/all_to_all | solution.py:60
  251.9 273.4 %all-reduce.4.cloned.1.call-start = ((), (), s32[]{:S(2)}) async-start(), calls=%async_computation.3 | async-start | bytes 1572864
  252.4 278.7 %copy-start.2 = (bf16[128,512]{1,0:T(8,128)(2,1)S(1)}, bf16[128,512]{1,0:T(8,128)(2,1)}, u32[]{:S(2)}) copy-start(bf16[128,512]{1,0:T(8,128)(2,1)} %param.18) | copy-start | bytes 393220
Sparse Core Ops, SparseCore 0:
  255.9 269.2 all-reduce.3
where the time goes:
time: 540 us; the launch traced here: 539 us
  waiting for transfers between devices  369 us (68%)
  local copies, waits for them, and re-layouts  58.7 us (11%)
  starting transfers between devices  43.3 us (8%)
  matrix products  35.8 us (7%)
  between operations  14.9 us (3%)
  blocking collectives  11.9 us (2%)
    unnamed x2, waiting for transfers between devices  269 us
    all_to_all x2, waiting for transfers between devices, transpose_hop(): lax.all_to_all(outgoing, 'wide', split_axis=0, concat_axis=0, tiled=True)  99.9 us
    scatter x2, local copies, waits for them, and re-layouts, transpose_hop(): outgoing = jnp.zeros((owner_count, block_rows, local_width), jnp.bfloat16...  38.7 us
    all_to_all x2, starting transfers between devices, transpose_hop(): lax.all_to_all(outgoing, 'wide', split_axis=0, concat_axis=0, tiled=True)  25.7 us
    dot_general x2, matrix products, transpose_hop(): jnp.einsum('trj,trd->tjd', pattern, picked, preferred_element_type=jnp.fl...  24 us
    all_to_all x1, starting transfers between devices, transpose_hop(): lax.all_to_all(slot_ids, 'wide', split_axis=0, concat_axis=0, tiled=True)  17.3 us
    all_gather x1, blocking collectives, on_device(): gated_full = lax.all_gather(gated, 'narrow', axis=1, tiled=True)  11.9 us
  transfers between devices with their start and end apart: 4, of which 2 were waited for; matrix products, arithmetic and copies ran while one was open for 9% of the time, Pallas kernels for 0%

commit v1 on v0

--- a/solution.py
+++ b/solution.py
@@ -2,6 +2,11 @@
 import jax.numpy as jnp
 from jax import lax
 from jax.sharding import PartitionSpec as P
+
+
+def exchange_gather(x, axis, d):
+    outgoing = jnp.stack([x] * lax.axis_size(axis))
+    return jnp.concatenate(lax.all_to_all(outgoing, axis, 0, 0), axis=d)
 
 
 def tile_pattern(tile_cols):
@@ -33,7 +38,7 @@
     row_blocks = node_count // block_rows
     owner_count = lax.axis_size("wide")
     gated = grad_out * relu_mask.astype(jnp.bfloat16)
-    gated_full = lax.all_gather(gated, "narrow", axis=1, tiled=True)
+    gated_full = exchange_gather(gated, "narrow", 1)
     row_scale = norm[:, None]
     slot_ids = jnp.full((owner_count, 1), -1.0, jnp.float32)
     slot_ids = slot_ids.at[tile_owner, 0].set(tile_block.astype(jnp.float32)).astype(jnp.bfloat16)

time: 540 us -> 534 us (0.989)
  blocking collectives: 11.9 us -> 0 us
    all_gather x1 -> x0, blocking collectives: 11.9 us -> none  [on_device(): gated_full = lax.all_gather(gated, 'narrow', axis=1, tiled=True)]
  transfers between devices with their start and end apart: 4 -> 5, of which waited for: 2 -> 2; matrix products, arithmetic and copies ran while one was open for 9% -> 10% of each run, Pallas kernels for 0% -> 0%
where the time goes in v1:
time: 534 us; the launch traced here: 533 us
  waiting for transfers between devices  370 us (69%)
  local copies, waits for them, and re-layouts  59.5 us (11%)
  starting transfers between devices  47.7 us (9%)
  matrix products  35.8 us (7%)
  between operations  14.9 us (3%)
    unnamed x2, waiting for transfers between devices  270 us
    all_to_all x2, waiting for transfers between devices, transpose_hop(): lax.all_to_all(outgoing, 'wide', split_axis=0, concat_axis=0, tiled=True)  99.9 us
    scatter x2, local copies, waits for them, and re-layouts, transpose_hop(): outgoing = jnp.zeros((owner_count, block_rows, local_width), jnp.bfloat16...  38.7 us
    all_to_all x2, starting transfers between devices, transpose_hop(): lax.all_to_all(outgoing, 'wide', split_axis=0, concat_axis=0, tiled=True)  25.8 us
    dot_general x2, matrix products, transpose_hop(): jnp.einsum('trj,trd->tjd', pattern, picked, preferred_element_type=jnp.fl...  24 us
    all_to_all x1, starting transfers between devices, transpose_hop(): lax.all_to_all(slot_ids, 'wide', split_axis=0, concat_axis=0, tiled=True)  17.4 us
  transfers between devices with their start and end apart: 5, of which 2 were waited for; matrix products, arithmetic and copies ran while one was open for 10% of the time, Pallas kernels for 0%

profile of v1, /device:TPU:24, one launch (start us, length us, event | category | flops | bytes accessed | tf_op | source)
XLA Modules:
  0.0 532.9 jit_solution(2614324023005099750)
XLA Ops:
  7.2 1.0 convert_multiply_fusion
  9.0 4.3 all-to-all-start
  15.3 1.0 scatter_custom_fusion
  17.0 3.4 fusion.18
  20.5 17.4 %all-to-all-start.1 = ((bf16[128,1,1]{2,1,0:T(2,128)(2,1)}), bf16[128,1,1]{2,1,0:T(2,128)(2,1)S(1)}, u32[]{:S(2)}, u32[]{:S(2)}) async-start(bf16[128,1,1]{2,1,0:T(2,128)(2,1)} %copy.29), calls=%async_computation.1 | async-start | bytes 131072 | tf_op jit(solution)/shard_map/all_to_all | solution.py:66
  37.8 0.9 fusion.7
  38.8 3.1 gather_fusion
  41.9 12.0 %convolution_convert_fusion.1 = bf16[128,128,128]{2,1,0:T(8,128)(2,1)} fusion(bf16[128,128,128]{2,1,0:T(8,128)(2,1)} %gather_fusion, s32[128,128]{1,0:T(8,128)S(1)} %bitcast.67, s32[128,128]{1,0:T(8,128)S(1)} %bitcast.69, s32[128,128]{1,0:T(8,128)S(1)} %bitcast.57, s32[128,128]{1,0:T(8,128)S(1)} %bitcast.59, s32[128,128]{1,0:T(8,128)S(1)} %bitcast.61, ...), kind=kOutput, calls=%fused_computation.19 | convolution fusion | flops 589299712 | bytes 8912896 | tf_op jit(solution)/shard_map/trj,trd->tjd/dot_general | solution.py:56
  53.9 3.0 broadcast.19.clone
  56.9 19.3 %scatter_fusion = bf16[128,128,128]{2,1,0:T(8,128)(2,1)} fusion(bf16[128,128,128]{2,1,0:T(8,128)(2,1)} %broadcast.19.clone, s32[128]{0:T(128)S(1)} %compare_select_fusion.1, bf16[128,128,128]{2,1,0:T(8,128)(2,1)} %convolution_convert_fusion.1), kind=kCustom, calls=%fused_computation.3 | custom fusion | bytes 12583424 | tf_op jit(solution)/shard_map/scatter | solution.py:62
  76.2 14.2 %all-to-all-start.2 = ((bf16[128,128,128]{2,1,0:T(8,128)(2,1)}), bf16[128,128,128]{2,1,0:T(8,128)(2,1)}, u32[]{:S(2)}, u32[]{:S(2)}) async-start(bf16[128,128,128]{2,1,0:T(8,128)(2,1)} %scatter_fusion), calls=%async_computation.2 | async-start | bytes 8388608 | tf_op jit(solution)/shard_map/all_to_all | solution.py:65
  90.5 1.0 reduce
  91.5 99.9 %all-to-all-done.2 = bf16[128,128,128]{2,1,0:T(8,128)(2,1)} async-done(((bf16[128,128,128]{2,1,0:T(8,128)(2,1)}), bf16[128,128,128]{2,1,0:T(8,128)(2,1)}, u32[]{:S(2)}, u32[]{:S(2)}) %all-to-all-start.2) | async-done | bytes 4194336 | tf_op jit(solution)/shard_map/all_to_all | solution.py:65
  191.4 4.5 fusion.2
  196.2 3.1 gather_fusion.1
  199.3 12.0 %convolution_convert_fusion = bf16[128,128,128]{2,1,0:T(8,128)(2,1)} fusion(bf16[128,128,128]{2,1,0:T(8,128)(2,1)} %gather_fusion.1, s32[128,128]{1,0:T(8,128)S(1)} %bitcast.68, s32[128,128]{1,0:T(8,128)S(1)} %bitcast.70, s32[128,128]{1,0:T(8,128)S(1)} %bitcast.58, s32[128,128]{1,0:T(8,128)S(1)} %bitcast.60, s32[128,128]{1,0:T(8,128)S(1)} %bitcast.62, ...), kind=kOutput, calls=%fused_computation.18 | convolution fusion | flops 589299712 | bytes 8912896 | tf_op jit(solution)/shard_map/trj,trd->tjd/dot_general | solution.py:56
  211.3 3.0 broadcast.19
  214.3 19.3 %scatter_fusion.1 = bf16[128,128,128]{2,1,0:T(8,128)(2,1)} fusion(bf16[128,128,128]{2,1,0:T(8,128)(2,1)} %broadcast.19, s32[128]{0:T(128)S(1)} %compare_select_fusion.1, bf16[128,128,128]{2,1,0:T(8,128)(2,1)} %convolution_convert_fusion), kind=kCustom, calls=%fused_computation.4 | custom fusion | bytes 12583424 | tf_op jit(solution)/shard_map/scatter | solution.py:62
  233.6 11.6 %all-to-all-start.3 = ((bf16[128,128,128]{2,1,0:T(8,128)(2,1)}), bf16[128,128,128]{2,1,0:T(8,128)(2,1)}, u32[]{:S(2)}, u32[]{:S(2)}) async-start(bf16[128,128,128]{2,1,0:T(8,128)(2,1)} %scatter_fusion.1), calls=%async_computation.3 | async-start | bytes 8388608 | tf_op jit(solution)/shard_map/all_to_all | solution.py:65
  246.2 0.9 pad_maximum_fusion
  247.1 1.3 dynamic-slice
  249.1 270.2 %all-reduce.4.cloned.1.call-done = f32[3,512,128]{2,1,0:T(8,128)} async-done(((f32[3,512,128]{2,1,0:T(8,128)}), f32[3,512,128]{2,1,0:T(8,128)}) %all-reduce.4.cloned.1.call-update) | async-done | bytes 786448
  519.3 1.3 constant_dynamic-slice_fusion
  520.6 4.5 fusion
  (35 shorter events, 5.8 us)
Async XLA Ops:
  7.2 30.7 %copy-start = (bf16[128,512]{1,0:T(8,128)(2,1)S(1)}, bf16[128,512]{1,0:T(8,128)(2,1)}, u32[]{:S(2)}) copy-start(bf16[128,512]{1,0:T(8,128)(2,1)} %param.20) | copy-start | bytes 393220
  9.0 11.5 %all-to-all-start = ((bf16[4,256,128]{1,2,0:T(8,128)(2,1)}), bf16[4,256,128]{1,2,0:T(8,128)(2,1)S(1)}, u32[]{:S(2)}, u32[]{:S(2)}) async-start(bf16[4,256,128]{1,2,0:T(8,128)(2,1)} %stack.19), calls=%async_computation | async-start | bytes 524288 | tf_op jit(solution)/shard_map/all_to_all | solution.py:9
  20.5 55.8 %all-to-all-start.1 = ((bf16[128,1,1]{2,1,0:T(2,128)(2,1)}), bf16[128,1,1]{2,1,0:T(2,128)(2,1)S(1)}, u32[]{:S(2)}, u32[]{:S(2)}) async-start(bf16[128,1,1]{2,1,0:T(2,128)(2,1)} %copy.29), calls=%async_computation.1 | async-start | bytes 131072 | tf_op jit(solution)/shard_map/all_to_all | solution.py:66
  76.2 115.1 %all-to-all-start.2 = ((bf16[128,128,128]{2,1,0:T(8,128)(2,1)}), bf16[128,128,128]{2,1,0:T(8,128)(2,1)}, u32[]{:S(2)}, u32[]{:S(2)}) async-start(bf16[128,128,128]{2,1,0:T(8,128)(2,1)} %scatter_fusion), calls=%async_computation.2 | async-start | bytes 8388608 | tf_op jit(solution)/shard_map/all_to_all | solution.py:65
  90.5 105.4 %copy-start.1 = (bf16[128,512]{1,0:T(8,128)(2,1)S(1)}, bf16[128,512]{1,0:T(8,128)(2,1)}, u32[]{:S(2)}) copy-start(bf16[128,512]{1,0:T(8,128)(2,1)} %param.19) | copy-start | bytes 393220
  90.5 105.4 %copy-start.6 = (f32[256]{0:T(256)S(1)}, f32[256]{0:T(256)}, u32[]{:S(2)}) copy-start(f32[256]{0:T(256)} %param.21) | copy-start | bytes 3076
  233.6 11.8 %copy-start.3 = (bf16[256,128]{1,0:T(8,128)(2,1)S(1)}, bf16[256,128]{1,0:T(8,128)(2,1)}, u32[]{:S(2)}) copy-start(bf16[256,128]{1,0:T(8,128)(2,1)} %param.17) | copy-start | bytes 196612
  233.6 12.1 %copy-start.4 = (bf16[256,128]{1,0:T(8,128)(2,1)S(1)}, bf16[256,128]{1,0:T(8,128)(2,1)}, u32[]{:S(2)}) copy-start(bf16[256,128]{1,0:T(8,128)(2,1)} %param.16) | copy-start | bytes 196612
  233.6 12.3 %copy-start.5 = (bf16[256,128]{1,0:T(8,128)(2,1)S(1)}, bf16[256,128]{1,0:T(8,128)(2,1)}, u32[]{:S(2)}) copy-start(bf16[256,128]{1,0:T(8,128)(2,1)} %param.15) | copy-start | bytes 196612
  233.6 287.0 %all-to-all-start.3 = ((bf16[128,128,128]{2,1,0:T(8,128)(2,1)}), bf16[128,128,128]{2,1,0:T(8,128)(2,1)}, u32[]{:S(2)}, u32[]{:S(2)}) async-start(bf16[128,128,128]{2,1,0:T(8,128)(2,1)} %scatter_fusion.1), calls=%async_computation.3 | async-start | bytes 8388608 | tf_op jit(solution)/shard_map/all_to_all | solution.py:65
  245.2 274.1 %all-reduce.4.cloned.1.call-start = ((), (), s32[]{:S(2)}) async-start(), calls=%async_computation.4 | async-start | bytes 1572864
  245.7 279.4 %copy-start.2 = (bf16[128,512]{1,0:T(8,128)(2,1)S(1)}, bf16[128,512]{1,0:T(8,128)(2,1)}, u32[]{:S(2)}) copy-start(bf16[128,512]{1,0:T(8,128)(2,1)} %param.18) | copy-start | bytes 393220
Sparse Core Ops, SparseCore 0:
  249.2 270.0 all-reduce.3
